TPU v7x, 128 devices: a whole 4x4x4 slice. The times are simulated.
128 devices in a mesh: seq: 32 (over x, z_lo, y), head: 2 (over core), dp: 2 (over z_hi).
Axes of the slice: x: 4, y: 4, z: 4 (z_hi: 2, z_lo: 2; z = z_hi * 2 + z_lo), core: 2. Of those that a mesh axis runs over, the one named last changes fastest.
Arguments:
- queries: bfloat16 [16384, 2048], P(('dp', 'seq'), 'head'), parts along dimension 0, may hold values from -32 to 32
- keys: bfloat16 [16384, 2048], P(('dp', 'seq'), 'head'), parts along dimension 0, may hold values from -32 to 32
- values: bfloat16 [16384, 2048], P(('dp', 'seq'), 'head'), parts along dimension 0, may hold values from -6 to 6
- out_grad: bfloat16 [16384, 4096], P(('dp', 'seq')), parts along dimension 0, may hold values from -6 to 6
- proj_weight: bfloat16 [4096, 2048], P(None, 'head'), may hold values from -0.09375 to 0.09375
- layout: int32 [64, 12], replicated, may hold values from -1 to 63, as said below
Outputs:
- query_grad: bfloat16 [16384, 2048], P(('dp', 'seq'), 'head'), parts along dimension 0
- key_grad: bfloat16 [16384, 2048], P(('dp', 'seq'), 'head'), parts along dimension 0
- value_grad: bfloat16 [16384, 2048], P(('dp', 'seq'), 'head'), parts along dimension 0
- proj_grad: float32 [8192, 2048], P(('dp', 'seq'), 'head'), parts along dimension 0
There are 2 independent parts, one for each index of `dp`. A program takes and returns all parts, laid end to end along the dimension named above; an argument that names none is the same for every part. Nothing has to cross between parts.
Inputs may be any that keep to these rules, and one draw needn't show every extreme that they name: `layout`: row i lists, in increasing order, some of the blocks j < i - 7 whose remainder modulo 16 equals one offset, below 8 and shared by all rows (the last row lists all of them), then the blocks max(0, i - w + 1) to i for a window w of its own between 1 and 8, and ends with -1 in the unused entries; a row whose block follows a block of that remainder has w = 8.
All inputs are finite; a program needn't handle non-finite values.
Results may differ from a plain program's by a relative error of at most 0.03.
Values may be sent and summed in bfloat16 or wider, within the bound.
A program may use at most 192 MiB of HBM per device.

v0:
```python
import jax
import jax.numpy as jnp
from jax import lax
from jax.sharding import PartitionSpec as P

HD = 128
BLK = 128
LOCAL = 8
STRIDE = 16


def passed_along(block, axis, distance):
    devices = range(lax.axis_size(axis))
    route = [(i - distance, i) for i in devices if i - distance in devices]
    return lax.ppermute(block, axis, route)


def broadcast(array, axis, root):
    mine = lax.axis_index(axis) == root
    return lax.psum(jnp.where(mine, array, jnp.zeros_like(array)), axis)


def listed(table_row, block_ids):
    return jnp.any(table_row[None, :] == block_ids[:, None], axis=1) & (block_ids >= 0)


def local(queries, keys, values, out_grad, proj_weight, layout):
    tok_dev = queries.shape[0]
    width = queries.shape[1]
    heads_here = width // HD
    blocks_dev = tok_dev // BLK
    block_count = layout.shape[0]
    summary_count = block_count // STRIDE
    score_scale = HD ** (-0.5)
    first_block = lax.axis_index("seq") * blocks_dev
    offset_block = layout[block_count - 1, 0] % STRIDE
    reach_back = (LOCAL - 2) // blocks_dev + 1
    span_blocks = [
        min(blocks_dev, LOCAL - 1 - hop_index * blocks_dev) for hop_index in range(reach_back)
    ]
    attn_grad = jnp.dot(out_grad, proj_weight, preferred_element_type=jnp.float32).astype(
        jnp.bfloat16
    )
    near_keys = []
    near_values = []
    for distance in range(reach_back, 0, -1):
        rows_needed = span_blocks[distance - 1] * BLK
        moved_keys, moved_values = passed_along(
            (keys[tok_dev - rows_needed :], values[tok_dev - rows_needed :]), "seq", distance
        )
        near_keys.append(moved_keys)
        near_values.append(moved_values)
    pool_keys = jnp.concatenate(near_keys + [keys], axis=0).reshape(-1, heads_here, HD)
    pool_values = jnp.concatenate(near_values + [values], axis=0).reshape(-1, heads_here, HD)

    def fetch_summary(scan_state, summary_index):
        block_id = summary_index * STRIDE + offset_block
        start_row = block_id % blocks_dev * BLK
        owner_rank = block_id // blocks_dev
        piece_keys = lax.dynamic_slice_in_dim(keys, start_row, BLK, 0)
        piece_values = lax.dynamic_slice_in_dim(values, start_row, BLK, 0)
        received = (
            broadcast(piece_keys, "seq", owner_rank),
            broadcast(piece_values, "seq", owner_rank),
        )
        return (scan_state, received)

    ignored, fetched = lax.scan(fetch_summary, None, jnp.arange(summary_count, dtype=jnp.int32))
    far_keys = fetched[0].reshape(summary_count * BLK, heads_here, HD)
    far_values = fetched[1].reshape(summary_count * BLK, heads_here, HD)
    far_ids = jnp.arange(summary_count, dtype=jnp.int32) * STRIDE + offset_block
    query_blocks = queries.reshape(blocks_dev, BLK, heads_here, HD)
    grad_blocks = attn_grad.reshape(blocks_dev, BLK, heads_here, HD)
    window_offsets = jnp.arange(LOCAL, dtype=jnp.int32)
    causal_local = jnp.arange(LOCAL * BLK)[None, :] <= (LOCAL - 1) * BLK + jnp.arange(BLK)[:, None]

    def query_step(scan_state, local_block):
        query_rows = query_blocks[local_block]
        grad_rows = grad_blocks[local_block]
        block_id = first_block + local_block
        table_row = layout[block_id]
        window_key_rows = lax.dynamic_slice_in_dim(pool_keys, local_block * BLK, LOCAL * BLK, 0)
        window_value_rows = lax.dynamic_slice_in_dim(pool_values, local_block * BLK, LOCAL * BLK, 0)
        window_ids = block_id - (LOCAL - 1) + window_offsets
        plain_window = (window_ids % STRIDE != offset_block) | (window_ids == block_id)
        local_allowed = (
            causal_local & jnp.repeat(listed(table_row, window_ids) & plain_window, BLK)[None, :]
        )
        far_allowed = jnp.repeat(listed(table_row, far_ids) & (far_ids < block_id), BLK)[None, :]
        near_scores = (
            jnp.einsum(
                "ahd,chd->hac", query_rows, window_key_rows, preferred_element_type=jnp.float32
            )
            * score_scale
        )
        far_scores = (
            jnp.einsum("ahd,chd->hac", query_rows, far_keys, preferred_element_type=jnp.float32)
            * score_scale
        )
        near_scores = jnp.where(local_allowed[None], near_scores, -jnp.inf)
        far_scores = jnp.where(far_allowed[None], far_scores, -jnp.inf)
        row_top = jnp.maximum(jnp.max(near_scores, axis=-1), jnp.max(far_scores, axis=-1))[
            ..., None
        ]
        row_total = jnp.sum(jnp.exp(near_scores - row_top), axis=-1, keepdims=True) + jnp.sum(
            jnp.exp(far_scores - row_top), axis=-1, keepdims=True
        )
        log_total = row_top + jnp.log(row_total)
        near_probs = jnp.exp(near_scores - log_total)
        far_probs = jnp.exp(far_scores - log_total)
        near_low = near_probs.astype(jnp.bfloat16)
        far_low = far_probs.astype(jnp.bfloat16)
        out_rows = (
            jnp.einsum(
                "hac,chd->ahd", near_low, window_value_rows, preferred_element_type=jnp.float32
            )
            + jnp.einsum("hac,chd->ahd", far_low, far_values, preferred_element_type=jnp.float32)
        ).astype(jnp.bfloat16)
        delta_rows = jnp.transpose(
            jnp.sum(out_rows.astype(jnp.float32) * grad_rows.astype(jnp.float32), axis=-1)
        )[..., None]
        near_dprob = jnp.einsum(
            "ahd,chd->hac", grad_rows, window_value_rows, preferred_element_type=jnp.float32
        )
        far_dprob = jnp.einsum(
            "ahd,chd->hac", grad_rows, far_values, preferred_element_type=jnp.float32
        )
        near_dscore = (score_scale * near_probs * (near_dprob - delta_rows)).astype(jnp.bfloat16)
        far_dscore = (score_scale * far_probs * (far_dprob - delta_rows)).astype(jnp.bfloat16)
        query_grad_rows = (
            jnp.einsum(
                "hac,chd->ahd", near_dscore, window_key_rows, preferred_element_type=jnp.float32
            )
            + jnp.einsum("hac,chd->ahd", far_dscore, far_keys, preferred_element_type=jnp.float32)
        ).astype(jnp.bfloat16)
        far_key_grad = scan_state[0] + jnp.einsum(
            "hac,ahd->chd", far_dscore, query_rows, preferred_element_type=jnp.float32
        )
        far_value_grad = scan_state[1] + jnp.einsum(
            "hac,ahd->chd", far_low, grad_rows, preferred_element_type=jnp.float32
        )
        start_row = local_block * BLK
        old_keys = lax.dynamic_slice_in_dim(scan_state[2], start_row, LOCAL * BLK, 0)
        old_values = lax.dynamic_slice_in_dim(scan_state[3], start_row, LOCAL * BLK, 0)
        new_keys = old_keys + jnp.einsum(
            "hac,ahd->chd", near_dscore, query_rows, preferred_element_type=jnp.float32
        )
        new_values = old_values + jnp.einsum(
            "hac,ahd->chd", near_low, grad_rows, preferred_element_type=jnp.float32
        )
        pool_key_grad = lax.dynamic_update_slice_in_dim(scan_state[2], new_keys, start_row, 0)
        pool_value_grad = lax.dynamic_update_slice_in_dim(scan_state[3], new_values, start_row, 0)
        new_state = (far_key_grad, far_value_grad, pool_key_grad, pool_value_grad)
        return (new_state, (out_rows, query_grad_rows, log_total[..., 0], delta_rows[..., 0]))

    far_zeros = jnp.zeros((summary_count * BLK, heads_here, HD), jnp.float32)
    pool_zeros = jnp.zeros((pool_keys.shape[0], heads_here, HD), jnp.float32)
    init_state = (far_zeros, far_zeros, pool_zeros, pool_zeros)
    state_out, scanned = lax.scan(query_step, init_state, jnp.arange(blocks_dev, dtype=jnp.int32))
    out_blocks, query_parts, log_blocks, delta_blocks = scanned
    attn_out = out_blocks.reshape(tok_dev, width)
    query_grad = query_parts.reshape(tok_dev, width)
    own_ids = first_block + jnp.arange(blocks_dev, dtype=jnp.int32)
    is_summary = own_ids % STRIDE == offset_block
    summary_slot = jnp.minimum(own_ids // STRIDE, summary_count - 1)
    summed = lax.psum((state_out[0], state_out[1]), "seq")
    far_key_sum = summed[0].reshape(summary_count, BLK, width)
    far_value_sum = summed[1].reshape(summary_count, BLK, width)
    far_key_add = jnp.take(far_key_sum, summary_slot, axis=0)
    far_value_add = jnp.take(far_value_sum, summary_slot, axis=0)
    own_start = (LOCAL - 1) * BLK
    key_grad = state_out[2][own_start:]
    value_grad = state_out[3][own_start:]
    pool_start = 0
    for distance in range(reach_back, 0, -1):
        rows_needed = span_blocks[distance - 1] * BLK
        back_keys, back_values = passed_along(
            (
                state_out[2][pool_start : pool_start + rows_needed],
                state_out[3][pool_start : pool_start + rows_needed],
            ),
            "seq",
            -distance,
        )
        key_grad = key_grad.at[tok_dev - rows_needed :].add(back_keys)
        value_grad = value_grad.at[tok_dev - rows_needed :].add(back_values)
        pool_start = pool_start + rows_needed
    key_total = key_grad.reshape(blocks_dev, BLK, width) + jnp.where(
        is_summary[:, None, None], far_key_add, 0.0
    )
    value_total = value_grad.reshape(blocks_dev, BLK, width) + jnp.where(
        is_summary[:, None, None], far_value_add, 0.0
    )
    proj_grad = lax.psum_scatter(
        lax.dot_general(
            out_grad, attn_out, (((0,), (0,)), ((), ())), preferred_element_type=jnp.float32
        ),
        "seq",
        scatter_dimension=0,
        tiled=True,
    )
    key_out = key_total.reshape(tok_dev, width).astype(jnp.bfloat16)
    value_out = value_total.reshape(tok_dev, width).astype(jnp.bfloat16)
    return (query_grad, key_out, value_out, proj_grad)


def solution(mesh):
    return jax.shard_map(
        local,
        mesh=mesh,
        in_specs=(
            P(("dp", "seq"), "head"),
            P(("dp", "seq"), "head"),
            P(("dp", "seq"), "head"),
            P(("dp", "seq"), None),
            P(None, "head"),
            P(),
        ),
        out_specs=(
            P(("dp", "seq"), "head"),
            P(("dp", "seq"), "head"),
            P(("dp", "seq"), "head"),
            P(("dp", "seq"), "head"),
        ),
        check_vma=False,
    )
```

profile of v0, /device:TPU:0, one launch (start us, length us, event | category | flops | bytes accessed | tf_op | source)
XLA Modules:
  0.0 2074.4 jit_solution(11944361138026221976)
XLA Ops:
  10.2 5.8 collective-permute-start.1
  16.0 4.7 collective-permute-start.2
  37.1 6.6 fusion.40
  43.7 1255.1 %while.53 = (s32[]{:T(128)}, bf16[4,128,1024]{2,1,0:T(8,128)(2,1)}, bf16[4,128,1024]{2,1,0:T(8,128)(2,1)}, s32[4]{0:T(128)S(1)}, s32[]{:T(128)}, /*index=5*/bf16...) while((s32[]{:T(128)}, bf16[4,128,1024]{2,1,0:T(8,128)(2,1)}, ...), condition=%wide.region_3.4_spmd, body=%wide.region_0.3_spmd.sunk | while | flops 524319 | bytes 5243400 | solution.py:68
  45.9 308.6 %all-reduce.9.cloned.1.call-done = (bf16[1,128,1024]{2,1,0:T(8,128)(2,1)}, bf16[1,128,1024]{2,1,0:T(8,128)(2,1)}) async-done(((bf16[1,128,1024]{2,1,0:T(8,128)(2,1)}, bf16[1,128,1024]{2,1,0:T(8,128)(2,1)}), (bf16[1,128,1024]{2,1,0:T(8,128)(2,1)}, bf16[1,128,1024]{2,1,0:T(8,128)(2,1)})) %all-reduce.9.cloned.1.call-update) | async-done | bytes 524304 | tf_op jit(solution)/shard_map/while/body/eval_jaxpr/psum | solution.py:20
  359.9 308.3 %all-reduce.9.cloned.1.call-done = (bf16[1,128,1024]{2,1,0:T(8,128)(2,1)}, bf16[1,128,1024]{2,1,0:T(8,128)(2,1)}) async-done(((bf16[1,128,1024]{2,1,0:T(8,128)(2,1)}, bf16[1,128,1024]{2,1,0:T(8,128)(2,1)}), (bf16[1,128,1024]{2,1,0:T(8,128)(2,1)}, bf16[1,128,1024]{2,1,0:T(8,128)(2,1)})) %all-reduce.9.cloned.1.call-update) | async-done | bytes 524304 | tf_op jit(solution)/shard_map/while/body/eval_jaxpr/psum | solution.py:20
  673.7 308.3 %all-reduce.9.cloned.1.call-done = (bf16[1,128,1024]{2,1,0:T(8,128)(2,1)}, bf16[1,128,1024]{2,1,0:T(8,128)(2,1)}) async-done(((bf16[1,128,1024]{2,1,0:T(8,128)(2,1)}, bf16[1,128,1024]{2,1,0:T(8,128)(2,1)}), (bf16[1,128,1024]{2,1,0:T(8,128)(2,1)}, bf16[1,128,1024]{2,1,0:T(8,128)(2,1)})) %all-reduce.9.cloned.1.call-update) | async-done | bytes 524304 | tf_op jit(solution)/shard_map/while/body/eval_jaxpr/psum | solution.py:20
  987.5 308.0 %all-reduce.9.cloned.1.call-done = (bf16[1,128,1024]{2,1,0:T(8,128)(2,1)}, bf16[1,128,1024]{2,1,0:T(8,128)(2,1)}) async-done(((bf16[1,128,1024]{2,1,0:T(8,128)(2,1)}, bf16[1,128,1024]{2,1,0:T(8,128)(2,1)}), (bf16[1,128,1024]{2,1,0:T(8,128)(2,1)}, bf16[1,128,1024]{2,1,0:T(8,128)(2,1)})) %all-reduce.9.cloned.1.call-update) | async-done | bytes 524304 | tf_op jit(solution)/shard_map/while/body/eval_jaxpr/psum | solution.py:20
  1327.2 4.4 copy.75
  1336.6 88.2 %while.54 = (s32[]{:T(128)}, f32[512,8,128]{0,2,1:T(8,128)}, f32[512,8,128]{0,2,1:T(8,128)}, f32[1152,8,128]{0,2,1:T(8,128)}, f32[1152,8,128]{0,2,1:T(8,128)}, /...) while((s32[]{:T(128)}, f32[512,8,128]{0,2,1:T(8,128)}, ...), condition=%wide.region_12.13_spmd.clone.clone.clone, body=%wide.region_4.12_spmd.clone.clone.clone.sunk | while | flops 2451831296 | bytes 213504784 | solution.py:159
  1365.1 5.0 fusion.104
  1372.0 3.9 fusion.106
  1400.5 3.5 bitcast_add_fusion.6
  1409.4 5.1 fusion.104
  1416.4 3.9 fusion.106
  1437.6 8.1 convolution_bitcast_fusion.2
  1459.2 9.6 collective-permute-done.12
  1470.1 7.1 collective-permute-done.8
  1478.5 9.2 collective-permute-done.15
  1494.6 8.0 collective-permute-done.13
  1507.8 23.1 %collective-permute-done.10 = f32[256,8,128]{0,2,1:T(8,128)} collective-permute-done((f32[256,8,128]{0,2,1:T(8,128)}, f32[256,8,128]{0,2,1:T(8,128)}, u32[]{:S(2)}, u32[]{:S(2)}) %collective-permute-start.10) | collective-permute-done | bytes 1048608 | tf_op jit(solution)/shard_map/ppermute | solution.py:15
  1530.9 72.0 %collective-permute-done.9 = f32[256,8,128]{0,2,1:T(8,128)} collective-permute-done((f32[256,8,128]{0,2,1:T(8,128)}, f32[256,8,128]{0,2,1:T(8,128)}, u32[]{:S(2)}, u32[]{:S(2)}) %collective-permute-start.9) | collective-permute-done | bytes 1048608 | tf_op jit(solution)/shard_map/ppermute | solution.py:15
  1609.2 250.2 %all-reduce.7.cloned.1.call-done = (f32[4,128,1024]{2,1,0:T(8,128)}, f32[4,128,1024]{2,1,0:T(8,128)}) async-done(((f32[4,128,1024]{2,1,0:T(8,128)}, f32[4,128,1024]{2,1,0:T(8,128)}), (f32[4,128,1024]{2,1,0:T(8,128)}, f32[4,128,1024]{2,1,0:T(8,128)})) %all-reduce.7.cloned.1.call-update) | async-done | bytes 4194320 | tf_op jit(solution)/shard_map/psum | solution.py:166
  1868.1 197.1 %reduce-scatter.2.cloned.1.call-done = f32[128,1024]{0,1:T(8,128)} async-done(((f32[4096,1024]{0,1:T(8,128)}), f32[128,1024]{0,1:T(8,128)}) %reduce-scatter.2.cloned.1.call-update) | async-done | bytes 524304 | tf_op jit(solution)/shard_map/reduce_scatter | solution.py:194
  (258 shorter events, 186.9 us)
Async XLA Ops:
  8.0 29.1 %copy-start = (bf16[256,4096]{1,0:T(8,128)(2,1)S(1)}, bf16[256,4096]{1,0:T(8,128)(2,1)}, u32[]{:S(2)}) copy-start(bf16[256,4096]{1,0:T(8,128)(2,1)} %param.43) | copy-start | bytes 6291460
  10.2 1302.5 %collective-permute-start.1 = (bf16[256,1024]{0,1:T(8,128)(2,1)}, bf16[256,1024]{0,1:T(8,128)(2,1)}, u32[]{:S(2)}, u32[]{:S(2)}) collective-permute-start(bf16[256,1024]{0,1:T(8,128)(2,1)} %copy.69), channel_id=1, source_target_pairs={{0,12},{4,16},{8,20},{12,24},{16,28},{20,32},{24,36},{28,40},{32,4... | collective-permute-start | bytes 1572872 | tf_op jit(solution)/shard_map/ppermute | solution.py:15
  16.0 1302.0 %collective-permute-start.2 = (bf16[256,1024]{0,1:T(8,128)(2,1)}, bf16[256,1024]{0,1:T(8,128)(2,1)}, u32[]{:S(2)}, u32[]{:S(2)}) collective-permute-start(bf16[256,1024]{0,1:T(8,128)(2,1)} %copy.69), channel_id=1, source_target_pairs={{0,8},{4,12},{8,16},{12,20},{16,24},{20,28},{24,32},{28,36},{32,40... | collective-permute-start | bytes 1572872 | tf_op jit(solution)/shard_map/ppermute | solution.py:15
  20.7 1299.3 %collective-permute-start.3 = (bf16[256,1024]{0,1:T(8,128)(2,1)}, bf16[256,1024]{0,1:T(8,128)(2,1)}, u32[]{:S(2)}, u32[]{:S(2)}) collective-permute-start(bf16[256,1024]{0,1:T(8,128)(2,1)} %copy.69), channel_id=1, source_target_pairs={{0,4},{4,8},{8,12},{12,16},{16,20},{20,24},{24,28},{28,32},{32,36}... | collective-permute-start | bytes 1572872 | tf_op jit(solution)/shard_map/ppermute | solution.py:15
  25.3 1281.0 %collective-permute-start = (bf16[128,1024]{0,1:T(8,128)(2,1)}, bf16[128,1024]{0,1:T(8,128)(2,1)}, u32[]{:S(2)}, u32[]{:S(2)}) collective-permute-start(bf16[128,1024]{0,1:T(8,128)(2,1)} %slice.222), channel_id=1, source_target_pairs={{0,16},{4,20},{8,24},{12,28},{16,32},{20,36},{24,40},{28,44},{32,4... | collective-permute-start | bytes 786440 | tf_op jit(solution)/shard_map/ppermute | solution.py:15
  29.0 1281.7 %collective-permute-start.4 = (bf16[128,1024]{1,0:T(8,128)(2,1)}, bf16[128,1024]{1,0:T(8,128)(2,1)S(1)}, u32[]{:S(2)}, u32[]{:S(2)}) collective-permute-start(bf16[128,1024]{1,0:T(8,128)(2,1)} %slice.205), channel_id=1, source_target_pairs={{0,16},{4,20},{8,24},{12,28},{16,32},{20,36},{24,40},{28,44},{32,4... | collective-permute-start | bytes 786440 | tf_op jit(solution)/shard_map/ppermute | solution.py:15
  43.7 310.8 %all-reduce.9.cloned.1.call-start = ((), (), s32[]{:S(2)}) async-start(), calls=%async_computation.3 | async-start | bytes 1048576 | tf_op jit(solution)/shard_map/while/body/eval_jaxpr/psum | solution.py:20
  357.8 310.4 %all-reduce.9.cloned.1.call-start = ((), (), s32[]{:S(2)}) async-start(), calls=%async_computation.3 | async-start | bytes 1048576 | tf_op jit(solution)/shard_map/while/body/eval_jaxpr/psum | solution.py:20
  671.6 310.4 %all-reduce.9.cloned.1.call-start = ((), (), s32[]{:S(2)}) async-start(), calls=%async_computation.3 | async-start | bytes 1048576 | tf_op jit(solution)/shard_map/while/body/eval_jaxpr/psum | solution.py:20
  985.4 310.1 %all-reduce.9.cloned.1.call-start = ((), (), s32[]{:S(2)}) async-start(), calls=%async_computation.3 | async-start | bytes 1048576 | tf_op jit(solution)/shard_map/while/body/eval_jaxpr/psum | solution.py:20
  1298.9 560.5 %all-reduce.7.cloned.1.call-start = ((), (), s32[]{:S(2)}) async-start(), calls=%async_computation.2 | async-start | bytes 8388608 | tf_op jit(solution)/shard_map/psum | solution.py:166
  1306.2 17.6 collective-permute-start.5
  1310.7 14.0 collective-permute-start.6
  1312.7 12.8 collective-permute-start.7
  1436.6 628.6 %reduce-scatter.2.cloned.1.call-start = ((), (), s32[]{:S(2)}) async-start(), calls=%async_computation.1 | async-start | bytes 17301504 | tf_op jit(solution)/shard_map/reduce_scatter | solution.py:194
  1448.5 39.2 %collective-permute-start.15 = (f32[256,8,128]{0,2,1:T(8,128)S(1)}, f32[256,8,128]{0,2,1:T(8,128)S(1)}, u32[]{:S(2)}, u32[]{:S(2)}) collective-permute-start(f32[256,8,128]{0,2,1:T(8,128)S(1)} %get-tuple-element.786), channel_id=1, source_target_pairs={{4,0},{8,4},{12,8},{16,12},{20,16},{24,20},{28,24},{32,28},{36,32}... | collective-permute-start | bytes 3145736 | tf_op jit(solution)/shard_map/ppermute | solution.py:15
  1450.9 17.9 collective-permute-start.12
  1453.3 23.9 %collective-permute-start.8 = (f32[128,8,128]{0,2,1:T(8,128)S(1)}, f32[128,8,128]{0,2,1:T(8,128)S(1)}, u32[]{:S(2)}, u32[]{:S(2)}) collective-permute-start(f32[128,8,128]{0,2,1:T(8,128)S(1)} %slice.208), channel_id=1, source_target_pairs={{16,0},{20,4},{24,8},{28,12},{32,16},{36,20},{40,24},{44,28},{48,3... | collective-permute-start | bytes 1572872 | tf_op jit(solution)/shard_map/ppermute | solution.py:15
  1454.6 40.0 %collective-permute-start.14 = (f32[256,8,128]{0,2,1:T(8,128)S(1)}, f32[256,8,128]{0,2,1:T(8,128)S(1)}, u32[]{:S(2)}, u32[]{:S(2)}) collective-permute-start(f32[256,8,128]{0,2,1:T(8,128)S(1)} %get-tuple-element.787), channel_id=1, source_target_pairs={{8,0},{12,4},{16,8},{20,12},{24,16},{28,20},{32,24},{36,28},{40,32... | collective-permute-start | bytes 3145736 | tf_op jit(solution)/shard_map/ppermute | solution.py:15
  1455.9 33.1 %copy-start.20 = (bf16[2,128,8,128]{3,2,1,0:T(8,128)(2,1)S(1)}, bf16[2,128,8,128]{3,2,1,0:T(8,128)(2,1)}, u32[]{:S(2)}) copy-start(bf16[2,128,8,128]{3,2,1,0:T(8,128)(2,1)} %get-tuple-element.496) | copy-start | bytes 1572868
  1455.9 46.7 %collective-permute-start.13 = (f32[256,8,128]{0,2,1:T(8,128)S(1)}, f32[256,8,128]{0,2,1:T(8,128)S(1)}, u32[]{:S(2)}, u32[]{:S(2)}) collective-permute-start(f32[256,8,128]{0,2,1:T(8,128)S(1)} %get-tuple-element.784), channel_id=1, source_target_pairs={{12,0},{16,4},{20,8},{24,12},{28,16},{32,20},{36,24},{40,28},{44,3... | collective-permute-start | bytes 3145736 | tf_op jit(solution)/shard_map/ppermute | solution.py:15
  1468.8 39.0 %collective-permute-start.11 = (f32[256,8,128]{0,2,1:T(8,128)}, f32[256,8,128]{0,2,1:T(8,128)}, u32[]{:S(2)}, u32[]{:S(2)}) collective-permute-start(f32[256,8,128]{0,2,1:T(8,128)} %get-tuple-element.790), channel_id=1, source_target_pairs={{4,0},{8,4},{12,8},{16,12},{20,16},{24,20},{28,24},{32,28},{36,32}... | collective-permute-start | bytes 3145736 | tf_op jit(solution)/shard_map/ppermute | solution.py:15
  1477.2 53.7 %collective-permute-start.10 = (f32[256,8,128]{0,2,1:T(8,128)}, f32[256,8,128]{0,2,1:T(8,128)}, u32[]{:S(2)}, u32[]{:S(2)}) collective-permute-start(f32[256,8,128]{0,2,1:T(8,128)} %get-tuple-element.791), channel_id=1, source_target_pairs={{8,0},{12,4},{16,8},{20,12},{24,16},{28,20},{32,24},{36,28},{40,32... | collective-permute-start | bytes 3145736 | tf_op jit(solution)/shard_map/ppermute | solution.py:15
  1487.7 115.2 %collective-permute-start.9 = (f32[256,8,128]{0,2,1:T(8,128)}, f32[256,8,128]{0,2,1:T(8,128)}, u32[]{:S(2)}, u32[]{:S(2)}) collective-permute-start(f32[256,8,128]{0,2,1:T(8,128)} %get-tuple-element.788), channel_id=1, source_target_pairs={{12,0},{16,4},{20,8},{24,12},{28,16},{32,20},{36,24},{40,28},{44,3... | collective-permute-start | bytes 3145736 | tf_op jit(solution)/shard_map/ppermute | solution.py:15
  (43 other events, 216.3 us)
Sparse Core Ops, SparseCore 0:
  47.1 307.3 all-reduce.8
  361.2 307.0 all-reduce.8
  674.9 307.0 all-reduce.8
  988.4 307.0 all-reduce.8
Sparse Core Ops, SparseCore 1:
  1436.7 422.6 all-reduce.6
  1861.6 203.6 reduce-scatter.1
where the time goes:
time: 2080 us; the launch traced here: 2070 us
  waiting for transfers between devices  1810 us (87%)
  local copies, waits for them, and re-layouts  110 us (5%)
  matrix products  70.8 us (3%)
  starting transfers between devices  36.6 us (2%)
    psum x4, waiting for transfers between devices, broadcast(): return lax.psum(jnp.where(mine, array, jnp.zeros_like(array)), axis)  1230 us
    psum x1, waiting for transfers between devices, local(): summed = lax.psum((state_out[0], state_out[1]), 'seq')  250 us
    reduce_scatter x1, waiting for transfers between devices, local(): lax.psum_scatter(lax.dot_general(out_grad, attn_out, (((0,), (0,)), ((),...  197 us
    ppermute x16, waiting for transfers between devices, passed_along(): return lax.ppermute(block, axis, route)  134 us
  transfers between devices with their start and end apart: 22, of which 14 were waited for; matrix products, arithmetic and copies ran while one was open for 4% of the time, Pallas kernels for 0%

commit v1 on v0

--- a/solution.py
+++ b/solution.py
@@ -17,7 +17,7 @@
 
 def broadcast(array, axis, root):
     mine = lax.axis_index(axis) == root
-    return lax.psum(jnp.where(mine, array, jnp.zeros_like(array)), axis)
+    return jax.lax.all_gather(jnp.where(mine, array, jnp.zeros_like(array)), axis).sum(axis=0)
 
 
 def listed(table_row, block_ids):

time: 2080 us -> 2200 us (1.058)
  waiting for transfers between devices: 1810 us -> 1900 us
  other arithmetic: 15.4 us -> 66.1 us
    all_gather x0 -> x8, waiting for transfers between devices: none -> 1320 us  [broadcast(): jax.lax.all_gather(jnp.where(mine, array, jnp.zeros_like(array)), axis)]
    psum x4 -> x0, waiting for transfers between devices: 1230 us -> none  [broadcast(): return lax.psum(jnp.where(mine, array, jnp.zeros_like(array)), axis)]
    reduce_sum x0 -> x8, other arithmetic: none -> 44.4 us  [broadcast(): jax.lax.all_gather(jnp.where(mine, array, jnp.zeros_like(array)), axis)]
  transfers between devices with their start and end apart: 22 -> 26, of which waited for: 14 -> 17; matrix products, arithmetic and copies ran while one was open for 4% -> 6% of each run, Pallas kernels for 0% -> 0%
where the time goes in v1:
time: 2200 us
  waiting for transfers between devices  1900 us (86%)
  local copies, waits for them, and re-layouts  104 us (5%)
  matrix products  70.8 us (3%)
  other arithmetic  66.1 us (3%)
  starting transfers between devices  35.6 us (2%)
    all_gather x8, waiting for transfers between devices, broadcast(): jax.lax.all_gather(jnp.where(mine, array, jnp.zeros_like(array)), axis)  1320 us
    psum x1, waiting for transfers between devices, local(): summed = lax.psum((state_out[0], state_out[1]), 'seq')  253 us
    reduce_scatter x1, waiting for transfers between devices, local(): lax.psum_scatter(lax.dot_general(out_grad, attn_out, (((0,), (0,)), ((),...  197 us
    ppermute x16, waiting for transfers between devices, passed_along(): return lax.ppermute(block, axis, route)  122 us
    reduce_sum x8, other arithmetic, broadcast(): jax.lax.all_gather(jnp.where(mine, array, jnp.zeros_like(array)), axis)  44.4 us
  transfers between devices with their start and end apart: 26, of which 17 were waited for; matrix products, arithmetic and copies ran while one was open for 6% of the time, Pallas kernels for 0%

profile of v1, /device:TPU:0, one launch (start us, length us, event | category | flops | bytes accessed | tf_op | source)
XLA Modules:
  0.0 2199.6 jit_solution(7132508916437035482)
XLA Ops:
  10.2 5.8 collective-permute-start.1
  37.1 6.6 fusion.40
  43.7 1389.2 %while.54 = (s32[]{:T(128)}, bf16[4,128,1024]{2,1,0:T(8,128)(2,1)}, bf16[4,128,1024]{2,1,0:T(8,128)(2,1)}, s32[4]{0:T(128)S(1)}, s32[]{:T(128)}, /*index=5*/bf16...) while((s32[]{:T(128)}, bf16[4,128,1024]{2,1,0:T(8,128)(2,1)}, ...), condition=%wide.region_3.4_spmd, body=%wide.region_0.3_spmd.sunk | while | flops 8388639 | bytes 71303744 | solution.py:68
  47.6 166.8 %all-gather.9.cloned.1.call-done = bf16[4096,1024]{1,0:T(8,128)(2,1)} async-done(((bf16[128,1024]{1,0:T(8,128)(2,1)}), bf16[4096,1024]{1,0:T(8,128)(2,1)}) %all-gather.9.cloned.1.call-update) | async-done | bytes 8388624 | tf_op jit(solution)/shard_map/while/body/eval_jaxpr/all_gather | solution.py:20
  214.4 5.5 reduce_sum.77
  220.0 163.9 %all-gather.11.cloned.1.call-done = bf16[4096,1024]{1,0:T(8,128)(2,1)} async-done(((bf16[128,1024]{1,0:T(8,128)(2,1)}), bf16[4096,1024]{1,0:T(8,128)(2,1)}) %all-gather.11.cloned.1.call-update) | async-done | bytes 8388624 | tf_op jit(solution)/shard_map/while/body/eval_jaxpr/all_gather | solution.py:20
  383.9 5.5 reduce_sum.78
  394.7 167.1 %all-gather.9.cloned.1.call-done = bf16[4096,1024]{1,0:T(8,128)(2,1)} async-done(((bf16[128,1024]{1,0:T(8,128)(2,1)}), bf16[4096,1024]{1,0:T(8,128)(2,1)}) %all-gather.9.cloned.1.call-update) | async-done | bytes 8388624 | tf_op jit(solution)/shard_map/while/body/eval_jaxpr/all_gather | solution.py:20
  561.9 5.5 reduce_sum.77
  567.4 163.8 %all-gather.11.cloned.1.call-done = bf16[4096,1024]{1,0:T(8,128)(2,1)} async-done(((bf16[128,1024]{1,0:T(8,128)(2,1)}), bf16[4096,1024]{1,0:T(8,128)(2,1)}) %all-gather.11.cloned.1.call-update) | async-done | bytes 8388624 | tf_op jit(solution)/shard_map/while/body/eval_jaxpr/all_gather | solution.py:20
  742.0 167.1 %all-gather.9.cloned.1.call-done = bf16[4096,1024]{1,0:T(8,128)(2,1)} async-done(((bf16[128,1024]{1,0:T(8,128)(2,1)}), bf16[4096,1024]{1,0:T(8,128)(2,1)}) %all-gather.9.cloned.1.call-update) | async-done | bytes 8388624 | tf_op jit(solution)/shard_map/while/body/eval_jaxpr/all_gather | solution.py:20
  914.7 163.8 %all-gather.11.cloned.1.call-done = bf16[4096,1024]{1,0:T(8,128)(2,1)} async-done(((bf16[128,1024]{1,0:T(8,128)(2,1)}), bf16[4096,1024]{1,0:T(8,128)(2,1)}) %all-gather.11.cloned.1.call-update) | async-done | bytes 8388624 | tf_op jit(solution)/shard_map/while/body/eval_jaxpr/all_gather | solution.py:20
  1089.4 167.1 %all-gather.9.cloned.1.call-done = bf16[4096,1024]{1,0:T(8,128)(2,1)} async-done(((bf16[128,1024]{1,0:T(8,128)(2,1)}), bf16[4096,1024]{1,0:T(8,128)(2,1)}) %all-gather.9.cloned.1.call-update) | async-done | bytes 8388624 | tf_op jit(solution)/shard_map/while/body/eval_jaxpr/all_gather | solution.py:20
  1262.0 163.9 %all-gather.11.cloned.1.call-done = bf16[4096,1024]{1,0:T(8,128)(2,1)} async-done(((bf16[128,1024]{1,0:T(8,128)(2,1)}), bf16[4096,1024]{1,0:T(8,128)(2,1)}) %all-gather.11.cloned.1.call-update) | async-done | bytes 8388624 | tf_op jit(solution)/shard_map/while/body/eval_jaxpr/all_gather | solution.py:20
  1469.7 88.2 %while.55 = (s32[]{:T(128)}, f32[512,8,128]{0,2,1:T(8,128)}, f32[512,8,128]{0,2,1:T(8,128)}, f32[1152,8,128]{0,2,1:T(8,128)}, f32[1152,8,128]{0,2,1:T(8,128)}, /...) while((s32[]{:T(128)}, f32[512,8,128]{0,2,1:T(8,128)}, ...), condition=%wide.region_12.13_spmd.clone.clone.clone, body=%wide.region_4.12_spmd.clone.clone.clone.sunk | while | flops 2451831296 | bytes 213504784 | solution.py:159
  1570.7 8.1 convolution_bitcast_fusion.2
  1592.2 9.1 collective-permute-done.12
  1602.6 7.1 collective-permute-done.8
  1611.0 12.6 collective-permute-done.15
  1637.1 6.7 collective-permute-done.11
  1643.8 21.7 collective-permute-done.10
  1665.5 59.5 %collective-permute-done.9 = f32[256,8,128]{0,2,1:T(8,128)} collective-permute-done((f32[256,8,128]{0,2,1:T(8,128)}, f32[256,8,128]{0,2,1:T(8,128)}, u32[]{:S(2)}, u32[]{:S(2)}) %collective-permute-start.9) | collective-permute-done | bytes 1048608 | tf_op jit(solution)/shard_map/ppermute | solution.py:15
  1731.3 253.1 %all-reduce.3.cloned.1.call-done = (f32[4,128,1024]{2,1,0:T(8,128)}, f32[4,128,1024]{2,1,0:T(8,128)}) async-done(((f32[4,128,1024]{2,1,0:T(8,128)}, f32[4,128,1024]{2,1,0:T(8,128)}), (f32[4,128,1024]{2,1,0:T(8,128)}, f32[4,128,1024]{2,1,0:T(8,128)})) %all-reduce.3.cloned.1.call-update) | async-done | bytes 4194320 | tf_op jit(solution)/shard_map/psum | solution.py:166
  1993.1 197.1 %reduce-scatter.2.cloned.1.call-done = f32[128,1024]{0,1:T(8,128)} async-done(((f32[4096,1024]{0,1:T(8,128)}), f32[128,1024]{0,1:T(8,128)}) %reduce-scatter.2.cloned.1.call-update) | async-done | bytes 524304 | tf_op jit(solution)/shard_map/reduce_scatter | solution.py:194
  (280 shorter events, 244.4 us)
Async XLA Ops:
  10.2 1435.3 %collective-permute-start.1 = (bf16[256,1024]{0,1:T(8,128)(2,1)}, bf16[256,1024]{0,1:T(8,128)(2,1)}, u32[]{:S(2)}, u32[]{:S(2)}) collective-permute-start(bf16[256,1024]{0,1:T(8,128)(2,1)} %copy.69), channel_id=1, source_target_pairs={{0,12},{4,16},{8,20},{12,24},{16,28},{20,32},{24,36},{28,40},{32,4... | collective-permute-start | bytes 1572872 | tf_op jit(solution)/shard_map/ppermute | solution.py:15
  16.0 1435.2 %collective-permute-start.2 = (bf16[256,1024]{0,1:T(8,128)(2,1)}, bf16[256,1024]{0,1:T(8,128)(2,1)}, u32[]{:S(2)}, u32[]{:S(2)}) collective-permute-start(bf16[256,1024]{0,1:T(8,128)(2,1)} %copy.69), channel_id=1, source_target_pairs={{0,8},{4,12},{8,16},{12,20},{16,24},{20,28},{24,32},{28,36},{32,40... | collective-permute-start | bytes 1572872 | tf_op jit(solution)/shard_map/ppermute | solution.py:15
  20.7 1432.4 %collective-permute-start.3 = (bf16[256,1024]{0,1:T(8,128)(2,1)}, bf16[256,1024]{0,1:T(8,128)(2,1)}, u32[]{:S(2)}, u32[]{:S(2)}) collective-permute-start(bf16[256,1024]{0,1:T(8,128)(2,1)} %copy.69), channel_id=1, source_target_pairs={{0,4},{4,8},{8,12},{12,16},{16,20},{20,24},{24,28},{28,32},{32,36}... | collective-permute-start | bytes 1572872 | tf_op jit(solution)/shard_map/ppermute | solution.py:15
  25.3 1415.1 %collective-permute-start = (bf16[128,1024]{0,1:T(8,128)(2,1)}, bf16[128,1024]{0,1:T(8,128)(2,1)}, u32[]{:S(2)}, u32[]{:S(2)}) collective-permute-start(bf16[128,1024]{0,1:T(8,128)(2,1)} %slice.222), channel_id=1, source_target_pairs={{0,16},{4,20},{8,24},{12,28},{16,32},{20,36},{24,40},{28,44},{32,4... | collective-permute-start | bytes 786440 | tf_op jit(solution)/shard_map/ppermute | solution.py:15
  29.0 1414.4 %collective-permute-start.4 = (bf16[128,1024]{1,0:T(8,128)(2,1)}, bf16[128,1024]{1,0:T(8,128)(2,1)S(1)}, u32[]{:S(2)}, u32[]{:S(2)}) collective-permute-start(bf16[128,1024]{1,0:T(8,128)(2,1)} %slice.205), channel_id=1, source_target_pairs={{0,16},{4,20},{8,24},{12,28},{16,32},{20,36},{24,40},{28,44},{32,4... | collective-permute-start | bytes 786440 | tf_op jit(solution)/shard_map/ppermute | solution.py:15
  43.7 170.7 %all-gather.9.cloned.1.call-start = ((), (), s32[]{:S(2)}) async-start(), calls=%async_computation.3 | async-start | bytes 8650752 | tf_op jit(solution)/shard_map/while/body/eval_jaxpr/all_gather | solution.py:20
  46.8 337.1 %all-gather.11.cloned.1.call-start = ((), (), s32[]{:S(2)}) async-start(), calls=%async_computation.4 | async-start | bytes 8650752 | tf_op jit(solution)/shard_map/while/body/eval_jaxpr/all_gather | solution.py:20
  390.9 171.0 %all-gather.9.cloned.1.call-start = ((), (), s32[]{:S(2)}) async-start(), calls=%async_computation.3 | async-start | bytes 8650752 | tf_op jit(solution)/shard_map/while/body/eval_jaxpr/all_gather | solution.py:20
  393.9 337.3 %all-gather.11.cloned.1.call-start = ((), (), s32[]{:S(2)}) async-start(), calls=%async_computation.4 | async-start | bytes 8650752 | tf_op jit(solution)/shard_map/while/body/eval_jaxpr/all_gather | solution.py:20
  738.2 171.0 %all-gather.9.cloned.1.call-start = ((), (), s32[]{:S(2)}) async-start(), calls=%async_computation.3 | async-start | bytes 8650752 | tf_op jit(solution)/shard_map/while/body/eval_jaxpr/all_gather | solution.py:20
  741.2 337.3 %all-gather.11.cloned.1.call-start = ((), (), s32[]{:S(2)}) async-start(), calls=%async_computation.4 | async-start | bytes 8650752 | tf_op jit(solution)/shard_map/while/body/eval_jaxpr/all_gather | solution.py:20
  1085.5 171.0 %all-gather.9.cloned.1.call-start = ((), (), s32[]{:S(2)}) async-start(), calls=%async_computation.3 | async-start | bytes 8650752 | tf_op jit(solution)/shard_map/while/body/eval_jaxpr/all_gather | solution.py:20
  1088.5 337.4 %all-gather.11.cloned.1.call-start = ((), (), s32[]{:S(2)}) async-start(), calls=%async_computation.4 | async-start | bytes 8650752 | tf_op jit(solution)/shard_map/while/body/eval_jaxpr/all_gather | solution.py:20
  1433.0 551.4 %all-reduce.3.cloned.1.call-start = ((), (), s32[]{:S(2)}) async-start(), calls=%async_computation.2 | async-start | bytes 8388608 | tf_op jit(solution)/shard_map/psum | solution.py:166
  1440.4 16.5 collective-permute-start.5
  1569.7 620.5 %reduce-scatter.2.cloned.1.call-start = ((), (), s32[]{:S(2)}) async-start(), calls=%async_computation.1 | async-start | bytes 17301504 | tf_op jit(solution)/shard_map/reduce_scatter | solution.py:194
  1581.6 42.1 %collective-permute-start.15 = (f32[256,8,128]{0,2,1:T(8,128)S(1)}, f32[256,8,128]{0,2,1:T(8,128)S(1)}, u32[]{:S(2)}, u32[]{:S(2)}) collective-permute-start(f32[256,8,128]{0,2,1:T(8,128)S(1)} %get-tuple-element.811), channel_id=1, source_target_pairs={{4,0},{8,4},{12,8},{16,12},{20,16},{24,20},{28,24},{32,28},{36,32}... | collective-permute-start | bytes 3145736 | tf_op jit(solution)/shard_map/ppermute | solution.py:15
  1584.0 17.4 collective-permute-start.12
  1586.3 23.4 %collective-permute-start.8 = (f32[128,8,128]{0,2,1:T(8,128)S(1)}, f32[128,8,128]{0,2,1:T(8,128)S(1)}, u32[]{:S(2)}, u32[]{:S(2)}) collective-permute-start(f32[128,8,128]{0,2,1:T(8,128)S(1)} %slice.208), channel_id=1, source_target_pairs={{16,0},{20,4},{24,8},{28,12},{32,16},{36,20},{40,24},{44,28},{48,3... | collective-permute-start | bytes 1572872 | tf_op jit(solution)/shard_map/ppermute | solution.py:15
  1587.7 39.4 %collective-permute-start.14 = (f32[256,8,128]{0,2,1:T(8,128)S(1)}, f32[256,8,128]{0,2,1:T(8,128)S(1)}, u32[]{:S(2)}, u32[]{:S(2)}) collective-permute-start(f32[256,8,128]{0,2,1:T(8,128)S(1)} %get-tuple-element.812), channel_id=1, source_target_pairs={{8,0},{12,4},{16,8},{20,12},{24,16},{28,20},{32,24},{36,28},{40,32... | collective-permute-start | bytes 3145736 | tf_op jit(solution)/shard_map/ppermute | solution.py:15
  1589.0 44.0 %collective-permute-start.13 = (f32[256,8,128]{0,2,1:T(8,128)S(1)}, f32[256,8,128]{0,2,1:T(8,128)S(1)}, u32[]{:S(2)}, u32[]{:S(2)}) collective-permute-start(f32[256,8,128]{0,2,1:T(8,128)S(1)} %get-tuple-element.809), channel_id=1, source_target_pairs={{12,0},{16,4},{20,8},{24,12},{28,16},{32,20},{36,24},{40,28},{44,3... | collective-permute-start | bytes 3145736 | tf_op jit(solution)/shard_map/ppermute | solution.py:15
  1601.3 42.5 %collective-permute-start.11 = (f32[256,8,128]{0,2,1:T(8,128)}, f32[256,8,128]{0,2,1:T(8,128)}, u32[]{:S(2)}, u32[]{:S(2)}) collective-permute-start(f32[256,8,128]{0,2,1:T(8,128)} %get-tuple-element.815), channel_id=1, source_target_pairs={{4,0},{8,4},{12,8},{16,12},{20,16},{24,20},{28,24},{32,28},{36,32}... | collective-permute-start | bytes 3145736 | tf_op jit(solution)/shard_map/ppermute | solution.py:15
  1609.7 55.8 %collective-permute-start.10 = (f32[256,8,128]{0,2,1:T(8,128)}, f32[256,8,128]{0,2,1:T(8,128)}, u32[]{:S(2)}, u32[]{:S(2)}) collective-permute-start(f32[256,8,128]{0,2,1:T(8,128)} %get-tuple-element.816), channel_id=1, source_target_pairs={{8,0},{12,4},{16,8},{20,12},{24,16},{28,20},{32,24},{36,28},{40,32... | collective-permute-start | bytes 3145736 | tf_op jit(solution)/shard_map/ppermute | solution.py:15
  1623.6 101.4 %collective-permute-start.9 = (f32[256,8,128]{0,2,1:T(8,128)}, f32[256,8,128]{0,2,1:T(8,128)}, u32[]{:S(2)}, u32[]{:S(2)}) collective-permute-start(f32[256,8,128]{0,2,1:T(8,128)} %get-tuple-element.813), channel_id=1, source_target_pairs={{12,0},{16,4},{20,8},{24,12},{28,16},{32,20},{36,24},{40,28},{44,3... | collective-permute-start | bytes 3145736 | tf_op jit(solution)/shard_map/ppermute | solution.py:15
  (46 other events, 299.5 us)
Sparse Core Ops, SparseCore 0:
  46.9 167.5 all-gather.8
  216.1 167.7 all-gather.10
  394.0 167.7 all-gather.8
  563.4 167.7 all-gather.10
  741.3 167.7 all-gather.8
  910.7 167.7 all-gather.10
  1088.6 167.7 all-gather.8
  1258.1 167.7 all-gather.10
Sparse Core Ops, SparseCore 1:
  1569.7 414.5 all-reduce.2
  1986.6 203.5 reduce-scatter.1
